TPU v7x, 32 devices: a whole 2x2x4 slice. The times are simulated.
32 devices in a mesh: grp: 2 (over y), tm: 8 (over z, x), space: 2 (over core).
Axes of the slice: x: 2, y: 2, z: 4, core: 2. Of those that a mesh axis runs over, the one named last changes fastest.
Arguments:
- tokens: bfloat16 [16, 24, 64, 1024], P(('grp', 'tm'), 'space'), parts along dimension 0, may hold values from -28 to 28
- gains: float32 [2, 1024], replicated, may hold values from 0.5 to 2
- qkv_weights: bfloat16 [2, 1024, 1536], replicated, may hold values from -1.125 to 1.125
- out_weights: bfloat16 [2, 512, 1024], replicated, may hold values from -0.25 to 0.25
Outputs:
- video_out: bfloat16 [16, 24, 64, 1024], P(('grp', 'tm'), 'space'), parts along dimension 0
There are 2 independent parts, one for each index of `grp`. A program takes and returns all parts, laid end to end along the dimension named above; an argument that names none is the same for every part. Nothing has to cross between parts.
All inputs are finite; a program needn't handle non-finite values.
Results may differ from a plain program's by a relative error of at most 0.007.
Values may be sent and summed in bfloat16 or wider, within the bound.
No kernel may reach another device: no remote copies, remote signals or barrier semaphores. Data moves between devices by JAX's collectives and lax.ppermute only.
A program may use at most 64 MiB of HBM per device.

v0:
```python
import jax
import jax.numpy as jnp
from jax import lax
from jax.sharding import PartitionSpec as P

HEADS = 8
HEAD = 64


def block_groups(groups, length):
    target = max(1, 512 // length)
    chosen = 1
    for candidate in range(1, min(groups, target) + 1):
        if groups % candidate == 0:
            chosen = candidate
    return chosen


def attend(tokens, length, gain_row, qkv_weight, out_weight):
    tok_count, feat_count = tokens.shape
    inner_width = out_weight.shape[0]
    stream = tokens.astype(jnp.float32)
    normed = (
        stream * lax.rsqrt(jnp.mean(stream * stream, axis=-1, keepdims=True) + 1e-06) * gain_row
    ).astype(jnp.bfloat16)
    projected = jnp.dot(normed, qkv_weight, preferred_element_type=jnp.float32).astype(jnp.bfloat16)
    per_block = block_groups(tok_count // length, length) * length
    blocks = tok_count // per_block
    shaped = projected.reshape(blocks, per_block, 3, HEADS, HEAD)
    scores = jnp.einsum(
        "bqhd,bkhd->bhqk", shaped[:, :, 0], shaped[:, :, 1], preferred_element_type=jnp.float32
    ) * HEAD ** (-0.5)
    group_ids = jnp.arange(per_block) // length
    same_group = group_ids[:, None] == group_ids[None, :]
    scores = jnp.where(same_group, scores, -1e30)
    row_max = jnp.max(scores, axis=-1, keepdims=True)
    raised = jnp.exp(scores - row_max)
    weights = (raised / jnp.sum(raised, axis=-1, keepdims=True)).astype(jnp.bfloat16)
    mixture = jnp.einsum(
        "bhqk,bkhd->bqhd", weights, shaped[:, :, 2], preferred_element_type=jnp.float32
    ).astype(jnp.bfloat16)
    mixture = mixture.reshape(tok_count, inner_width)
    update = jnp.dot(mixture, out_weight, preferred_element_type=jnp.float32)
    return (stream + update).astype(jnp.bfloat16)


def shards(tokens, gains, qkv_weights, out_weights):
    spread = lax.axis_size("space")
    frame_count = lax.axis_size("tm")
    frame_tokens = tokens[0]
    row_count, col_count, feat_count = frame_tokens.shape
    half_cols = col_count // spread
    transposed = jnp.transpose(frame_tokens, (1, 0, 2)).reshape(
        spread, half_cols, row_count, feat_count
    )
    piece = lax.all_to_all(transposed, "space", split_axis=0, concat_axis=2, tiled=True)
    col_items = piece.shape[1]
    height_n = piece.shape[2]
    flat = piece.reshape(col_items * height_n, feat_count)
    done = attend(flat, height_n, gains[0], qkv_weights[0], out_weights[0])
    columns_done = done.reshape(1, col_items, height_n, feat_count)
    regrouped = columns_done.reshape(half_cols, spread, row_count, feat_count).transpose(0, 2, 1, 3)
    span = col_count * row_count // frame_count
    regrouped = regrouped.reshape(frame_count, span, 1, feat_count)
    piece = lax.all_to_all(regrouped, "tm", split_axis=0, concat_axis=2, tiled=True)
    pos_items = piece.shape[1]
    frame_n = piece.shape[2]
    flat = piece.reshape(pos_items * frame_n, feat_count)
    done = attend(flat, frame_n, gains[1], qkv_weights[1], out_weights[1])
    timed = done.reshape(1, pos_items, frame_n, feat_count)
    paired = timed.reshape(span // spread, spread, frame_count, feat_count).transpose(0, 2, 1, 3)
    paired = paired.reshape(span // spread, frame_count * spread, feat_count)
    back_rows = lax.all_to_all(paired, ("tm", "space"), split_axis=1, concat_axis=0, tiled=True)
    back_rows = back_rows.reshape(frame_count, spread, span // spread, feat_count).transpose(
        1, 0, 2, 3
    )
    restored = back_rows.reshape(col_count, row_count, feat_count)
    return jnp.transpose(restored, (1, 0, 2))[None]


def solution(mesh):
    return jax.shard_map(
        shards,
        mesh=mesh,
        in_specs=(P(("grp", "tm"), "space", None, None), P(), P(), P()),
        out_specs=P(("grp", "tm"), "space", None, None),
        check_vma=False,
    )
```

profile of v0, /device:TPU:1, one launch (start us, length us, event | category | flops | bytes accessed | tf_op | source)
XLA Modules:
  0.0 207.1 jit_solution(540313732590014101)
XLA Ops:
  0.0 2.7 %copy.114 = bf16[2,32,12,1024]{3,1,2,0:T(8,128)(2,1)} copy(bf16[2,32,12,1024]{3,1,0,2:T(8,128)(2,1)} %bitcast.161) | data formatting | bytes 3145728 | tf_op jit(solution)/shard_map/reshape | solution.py:53
  2.7 0.0 copy-start.3
  2.7 3.8 %all-to-all-start = ((bf16[2,32,12,1024]{3,1,2,0:T(8,128)(2,1)}), bf16[2,32,12,1024]{3,1,2,0:T(8,128)(2,1)S(1)}, u32[]{:S(2)}, u32[]{:S(2)}) async-start(bf16[2,32,12,1024]{3,1,2,0:T(8,128)(2,1)} %copy.114), calls=%async_computation | async-start | bytes 3145728 | tf_op jit(solution)/shard_map/all_to_all | solution.py:56
  6.6 2.1 %all-to-all-done = bf16[2,32,12,1024]{3,1,2,0:T(8,128)(2,1)S(1)} async-done(((bf16[2,32,12,1024]{3,1,2,0:T(8,128)(2,1)}), bf16[2,32,12,1024]{3,1,2,0:T(8,128)(2,1)S(1)}, u32[]{:S(2)}, u32[]{:S(2)}) %all-to-all-start) | async-done | bytes 1572896 | tf_op jit(solution)/shard_map/all_to_all | solution.py:56
  8.7 0.4 multiply_reduce_fusion
  9.1 0.0 copy-done.3
  9.1 0.4 multiply_convert_fusion
  9.5 2.2 %copy.116 = bf16[1,32,2,12,1024]{4,3,2,1,0:T(8,128)(2,1)} copy(bf16[1,32,2,12,1024]{4,1,3,2,0:T(8,128)(2,1)S(1)} %multiply_convert_fusion) | data formatting | bytes 3145728 | tf_op jit(solution)/shard_map/convert_element_type | solution.py:25
  11.8 2.5 %convert_element_type.84 = bf16[768,1024]{1,0:T(8,128)(2,1)S(1)} reshape(bf16[1,32,2,12,1024]{4,3,2,1,0:T(8,128)(2,1)} %copy.116) | data formatting | bytes 3145728 | tf_op jit(solution)/shard_map/convert_element_type | solution.py:25
  14.3 5.7 %convolution_convert_fusion.1 = bf16[768,1536]{1,0:T(8,128)(2,1)} fusion(bf16[768,1024]{1,0:T(8,128)(2,1)S(1)} %convert_element_type.84, bf16[2,1024,1536]{2,1,0:T(8,128)(2,1)} %param.6), kind=kOutput, calls=%fused_computation.23 | convolution fusion | flops 2417098752 | bytes 7077888 | tf_op jit(solution)/shard_map/dot_general | solution.py:26
  20.0 6.9 %reshape.162 = bf16[2,384,3,8,64]{4,3,2,1,0:T(8,128)(2,1)} reshape(bf16[768,1536]{1,0:T(8,128)(2,1)} %convolution_convert_fusion.1) | data formatting | bytes 4718592 | tf_op jit(solution)/shard_map/reshape | solution.py:29
  26.9 4.3 %fusion.75 = (bf16[2,384,1,8,64]{4,3,2,1,0:T(8,128)(2,1)S(1)}, bf16[2,384,1,8,64]{4,3,2,1,0:T(8,128)(2,1)}, bf16[2,384,1,8,64]{4,3,2,1,0:T(8,128)(2,1)}) fusion(bf16[2,384,3,8,64]{4,3,2,1,0:T(8,128)(2,1)} %reshape.162), kind=kLoop, calls=%fused_computation.86 | loop fusion | bytes 4718592 | tf_op jit(solution)/shard_map/slice | solution.py:40
  31.3 2.7 %copy.144 = bf16[2,384,1,8,64]{1,4,3,0,2:T(8,128)(2,1)} copy(bf16[2,384,1,8,64]{4,3,2,1,0:T(8,128)(2,1)} %get-tuple-element.9) | data formatting | bytes 1572864
  34.0 2.7 %copy.145 = bf16[2,384,1,8,64]{1,4,3,0,2:T(8,128)(2,1)} copy(bf16[2,384,1,8,64]{4,3,2,1,0:T(8,128)(2,1)} %get-tuple-element.10) | data formatting | bytes 1572864
  36.7 0.1 broadcast_compare_fusion.1
  36.8 1.7 copy.143
  38.5 0.0 copy-start
  38.6 8.2 %fusion.77 = (f32[2,8,384]{2,1,0:T(8,128)S(1)}, f32[2,8,384,384]{2,3,1,0:T(8,128)}) fusion(pred[384,384]{0,1:T(8,128)(4,1)S(1)} %broadcast_compare_fusion.1, bf16[2,384,1,8,64]{1,4,3,0,2:T(8,128)(2,1)} %copy.145, bf16[2,384,1,8,64]{1,4,3,0,2:T(8,128)(2,1)} %copy.144), kind=kOutput, calls=%fused_computation.88 | convolution fusion | flops 311427456 | bytes 11182080 | tf_op jit(solution)/shard_map/sub | solution.py:37
  46.7 0.0 copy-done
  46.8 4.5 %fusion.30 = bf16[2,384,8,64]{1,3,2,0:T(8,128)(2,1)S(1)} fusion(f32[2,8,384,384]{2,3,1,0:T(8,128)} %get-tuple-element.14, f32[2,8,384]{2,1,0:T(8,128)S(1)} %get-tuple-element.13, bf16[2,384,1,8,64]{1,4,3,0,2:T(8,128)(2,1)S(1)} %copy-done), kind=kOutput, calls=%fused_computation.44 | convolution fusion | flops 307101696 | bytes 11034624 | tf_op jit(solution)/shard_map/bhqk,bkhd->bqhd/dot_general | solution.py:39
  51.3 0.8 copy.122
  52.1 1.0 copy.149
  53.1 0.4 convert_bitcast_fusion.2
  53.5 3.8 %copy.115 = f32[1,32,2,12,1024]{4,3,2,1,0:T(8,128)} copy(f32[1,32,2,12,1024]{4,1,3,2,0:T(8,128)S(1)} %convert_bitcast_fusion.2) | data formatting | bytes 6291456 | tf_op jit(solution)/shard_map/convert_element_type | solution.py:22
  57.3 3.0 %reshape.156 = f32[768,1024]{1,0:T(8,128)S(1)} reshape(f32[1,32,2,12,1024]{4,3,2,1,0:T(8,128)} %copy.115) | data formatting | bytes 6291456 | tf_op jit(solution)/shard_map/convert_element_type | solution.py:22
  60.3 3.6 %add_convert_fusion = bf16[768,1024]{1,0:T(8,128)(2,1)} fusion(f32[768,1024]{1,0:T(8,128)S(1)} %reshape.156, bf16[768,512]{0,1:T(8,128)(2,1)} %bitcast.158, bf16[2,512,1024]{2,1,0:T(8,128)(2,1)} %param.7), kind=kOutput, calls=%fused_computation.33 | convolution fusion | flops 806879232 | bytes 6553600 | tf_op jit(solution)/shard_map/dot_general | solution.py:43
  63.9 2.5 %reshape_reshape.6 = bf16[32,2,12,1024]{3,2,1,0:T(8,128)(2,1)S(1)} reshape(bf16[768,1024]{1,0:T(8,128)(2,1)} %add_convert_fusion) | data formatting | bytes 3145728 | tf_op jit(solution)/shard_map/reshape;reshape | solution.py:62
  66.5 2.8 %copy.123 = bf16[32,12,2,1024]{3,2,1,0:T(2,128)(2,1)} copy(bf16[32,12,2,1024]{3,1,2,0:T(8,128)(2,1)S(1)} %bitcast.153) | data formatting | bytes 3145728 | tf_op jit(solution)/shard_map/transpose | solution.py:62
  69.3 3.7 %reshape.150 = bf16[8,96,1,1024]{3,1,0,2:T(8,128)(2,1)} reshape(bf16[32,12,2,1024]{3,2,1,0:T(2,128)(2,1)} %copy.123) | data formatting | bytes 3145728 | tf_op jit(solution)/shard_map/reshape | solution.py:64
  72.9 7.0 %all-to-all-start.1 = ((bf16[8,96,1,1024]{3,1,2,0:T(8,128)(2,1)}), bf16[8,96,1,1024]{3,1,2,0:T(8,128)(2,1)S(1)}, u32[]{:S(2)}, u32[]{:S(2)}) async-start(bf16[8,96,1,1024]{3,1,2,0:T(8,128)(2,1)} %bitcast.14), calls=%async_computation.1 | async-start | bytes 3145728 | tf_op jit(solution)/shard_map/all_to_all | solution.py:65
  79.9 0.1 broadcast_compare_fusion
  80.1 36.3 %all-to-all-done.1 = bf16[8,96,1,1024]{3,1,2,0:T(8,128)(2,1)S(1)} async-done(((bf16[8,96,1,1024]{3,1,2,0:T(8,128)(2,1)}), bf16[8,96,1,1024]{3,1,2,0:T(8,128)(2,1)S(1)}, u32[]{:S(2)}, u32[]{:S(2)}) %all-to-all-start.1) | async-done | bytes 1572896 | tf_op jit(solution)/shard_map/all_to_all | solution.py:65
  116.4 0.9 fusion.16
  117.3 0.1 copy.126
  117.4 0.1 copy.127
  117.5 7.4 %convolution_convert_fusion = bf16[768,1536]{1,0:T(8,128)(2,1)} fusion(bf16[2,1024,1536]{2,1,0:T(8,128)(2,1)} %param.6, f32[1024]{0:T(1024)S(1)} %bitcast.165, f32[96,8]{1,0:T(8,128)S(1)} %copy.127, bf16[8,96,1,1024]{3,1,2,0:T(8,128)(2,1)S(1)} %all-to-all-done.1), kind=kOutput, calls=%fused_computation.22 | convolution fusion | flops 2420244480 | bytes 7085056 | tf_op jit(solution)/shard_map/dot_general | solution.py:26
  124.9 6.9 %reshape.163 = bf16[2,384,3,8,64]{4,3,2,1,0:T(8,128)(2,1)} reshape(bf16[768,1536]{1,0:T(8,128)(2,1)} %convolution_convert_fusion) | data formatting | bytes 4718592 | tf_op jit(solution)/shard_map/reshape | solution.py:29
  131.8 4.3 %fusion.74 = (bf16[2,384,1,8,64]{4,3,2,1,0:T(8,128)(2,1)S(1)}, bf16[2,384,1,8,64]{4,3,2,1,0:T(8,128)(2,1)}, bf16[2,384,1,8,64]{4,3,2,1,0:T(8,128)(2,1)}) fusion(bf16[2,384,3,8,64]{4,3,2,1,0:T(8,128)(2,1)} %reshape.163), kind=kLoop, calls=%fused_computation.85 | loop fusion | bytes 4718592 | tf_op jit(solution)/shard_map/slice | solution.py:40
  136.2 2.7 %copy.147 = bf16[2,384,1,8,64]{1,4,3,0,2:T(8,128)(2,1)} copy(bf16[2,384,1,8,64]{4,3,2,1,0:T(8,128)(2,1)} %get-tuple-element.6) | data formatting | bytes 1572864
  138.9 2.7 %copy.148 = bf16[2,384,1,8,64]{1,4,3,0,2:T(8,128)(2,1)} copy(bf16[2,384,1,8,64]{4,3,2,1,0:T(8,128)(2,1)} %get-tuple-element.7) | data formatting | bytes 1572864
  141.6 1.7 copy.146
  143.3 0.0 copy-start.1
  143.3 8.2 %fusion.86 = (f32[2,8,384]{2,1,0:T(8,128)S(1)}, f32[2,8,384,384]{2,3,1,0:T(8,128)}) fusion(pred[384,384]{0,1:T(8,128)(4,1)S(1)} %broadcast_compare_fusion, bf16[2,384,1,8,64]{1,4,3,0,2:T(8,128)(2,1)} %copy.148, bf16[2,384,1,8,64]{1,4,3,0,2:T(8,128)(2,1)} %copy.147), kind=kOutput, calls=%fused_computation.89 | convolution fusion | flops 311427456 | bytes 11182080 | tf_op jit(solution)/shard_map/sub | solution.py:37
  151.5 0.0 copy-done.1
  151.5 4.5 %fusion.31 = bf16[2,384,8,64]{1,3,2,0:T(8,128)(2,1)S(1)} fusion(f32[2,8,384,384]{2,3,1,0:T(8,128)} %get-tuple-element.16, f32[2,8,384]{2,1,0:T(8,128)S(1)} %get-tuple-element.15, bf16[2,384,1,8,64]{1,4,3,0,2:T(8,128)(2,1)S(1)} %copy-done.1), kind=kOutput, calls=%fused_computation.45 | convolution fusion | flops 307101696 | bytes 11034624 | tf_op jit(solution)/shard_map/bhqk,bkhd->bqhd/dot_general | solution.py:39
  156.0 0.0 copy-start.2
  156.0 0.8 copy.133
  156.9 0.1 copy.150
  157.0 0.6 copy-done.2
  157.6 1.5 fusion.18
  159.2 0.9 copy.134
  160.0 41.4 %all_to_all.33 = bf16[48,16,1024]{2,0,1:T(8,128)(2,1)S(1)} all-to-all(bf16[48,16,1024]{2,0,1:T(8,128)(2,1)S(1)} %bitcast.155), channel_id=1, replica_groups=mesh['grp'=2,'tm'=8,'space'=2] {'tm','space'}, dimensions={1} | all-to-all | bytes 3145728 | tf_op jit(solution)/shard_map/all_to_all | solution.py:73
  201.4 1.3 copy.158
  202.7 2.4 %reshape.155 = bf16[64,12,1024]{2,1,0:T(8,128)(2,1)S(1)} reshape(bf16[2,8,48,1024]{3,2,1,0:T(8,128)(2,1)} %bitcast.157) | data formatting | bytes 3145728 | tf_op jit(solution)/shard_map/reshape | solution.py:77
  205.1 2.0 copy.136
  (5 shorter events, 0.0 us)
Async XLA Ops:
  2.7 6.3 %copy-start.3 = (f32[2,1024]{1,0:T(2,128)S(1)}, f32[2,1024]{1,0:T(2,128)}, u32[]{:S(2)}) copy-start(f32[2,1024]{1,0:T(2,128)} %param.5) | copy-start | bytes 24580
  2.7 5.9 %all-to-all-start = ((bf16[2,32,12,1024]{3,1,2,0:T(8,128)(2,1)}), bf16[2,32,12,1024]{3,1,2,0:T(8,128)(2,1)S(1)}, u32[]{:S(2)}, u32[]{:S(2)}) async-start(bf16[2,32,12,1024]{3,1,2,0:T(8,128)(2,1)} %copy.114), calls=%async_computation | async-start | bytes 3145728 | tf_op jit(solution)/shard_map/all_to_all | solution.py:56
  38.5 8.2 %copy-start = (bf16[2,384,1,8,64]{1,4,3,0,2:T(8,128)(2,1)S(1)}, bf16[2,384,1,8,64]{1,4,3,0,2:T(8,128)(2,1)}, u32[]{:S(2)}) copy-start(bf16[2,384,1,8,64]{1,4,3,0,2:T(8,128)(2,1)} %copy.143) | copy-start | bytes 2359300
  72.9 43.5 %all-to-all-start.1 = ((bf16[8,96,1,1024]{3,1,2,0:T(8,128)(2,1)}), bf16[8,96,1,1024]{3,1,2,0:T(8,128)(2,1)S(1)}, u32[]{:S(2)}, u32[]{:S(2)}) async-start(bf16[8,96,1,1024]{3,1,2,0:T(8,128)(2,1)} %bitcast.14), calls=%async_computation.1 | async-start | bytes 3145728 | tf_op jit(solution)/shard_map/all_to_all | solution.py:65
  143.3 8.2 %copy-start.1 = (bf16[2,384,1,8,64]{1,4,3,0,2:T(8,128)(2,1)S(1)}, bf16[2,384,1,8,64]{1,4,3,0,2:T(8,128)(2,1)}, u32[]{:S(2)}) copy-start(bf16[2,384,1,8,64]{1,4,3,0,2:T(8,128)(2,1)} %copy.146) | copy-start | bytes 2359300
  156.0 1.6 copy-start.2
where the time goes:
time: 208 us; the launch traced here: 207 us
  local copies, waits for them, and re-layouts  70.2 us (34%)
  matrix products  43.7 us (21%)
  blocking collectives  41.4 us (20%)
  waiting for transfers between devices  38.4 us (18%)
  starting transfers between devices  10.8 us (5%)
  other arithmetic  2.39 us (1%)
    all_to_all x1, blocking collectives, shards(): lax.all_to_all(paired, ('tm', 'space'), split_axis=1, concat_axis=0, tile...  41.4 us
    all_to_all x1, waiting for transfers between devices, shards(): lax.all_to_all(regrouped, 'tm', split_axis=0, concat_axis=2, tiled=True)  36.3 us
    sub x2, matrix products, attend(): raised = jnp.exp(scores - row_max)  16.4 us
    unnamed x16, local copies, waits for them, and re-layouts  16 us
    reshape x2, local copies, waits for them, and re-layouts, attend(): shaped = projected.reshape(blocks, per_block, 3, HEADS, HEAD)  13.9 us
    dot_general x2, matrix products, attend(): jnp.dot(normed, qkv_weight, preferred_element_type=jnp.float32)  13.1 us
    dot_general x2, matrix products, attend(): jnp.einsum('bhqk,bkhd->bqhd', weights, shaped[:, :, 2], preferred_element...  9.06 us
    slice x2, local copies, waits for them, and re-layouts, attend(): shaped[:, :, 2]  8.7 us
  transfers between devices with their start and end apart: 2, of which 2 were waited for; matrix products, arithmetic and copies ran while one was open for 0% of the time, Pallas kernels for 0%

commit v1 on v0

--- a/solution.py
+++ b/solution.py
@@ -5,6 +5,29 @@
 
 HEADS = 8
 HEAD = 64
+
+
+def split_up(array, dim, size):
+    dims = array.shape
+    blocks = array.reshape(*dims[:dim], size, dims[dim] // size, *dims[dim + 1 :])
+    return jnp.moveaxis(blocks, dim, 0)
+
+
+def in_order(blocks, dim):
+    blocks = jnp.moveaxis(blocks, 0, dim)
+    dims = blocks.shape
+    return blocks.reshape(*dims[:dim], dims[dim] * dims[dim + 1], *dims[dim + 2 :])
+
+
+def exchange_in_pairs(value, axis, split_dim, concat_dim):
+    size, here = (lax.axis_size(axis), lax.axis_index(axis))
+    blocks = split_up(value, split_dim, size)
+    gathered = [blocks[here]]
+    for hop in range(1, size):
+        sent = blocks[here ^ hop]
+        gathered.append(lax.ppermute(sent, axis, [(i, i ^ hop) for i in range(size)]))
+    blocks = jnp.stack(gathered)[here ^ jnp.arange(size)]
+    return in_order(blocks, concat_dim)
 
 
 def block_groups(groups, length):
@@ -62,7 +85,7 @@
     regrouped = columns_done.reshape(half_cols, spread, row_count, feat_count).transpose(0, 2, 1, 3)
     span = col_count * row_count // frame_count
     regrouped = regrouped.reshape(frame_count, span, 1, feat_count)
-    piece = lax.all_to_all(regrouped, "tm", split_axis=0, concat_axis=2, tiled=True)
+    piece = exchange_in_pairs(regrouped, "tm", 0, 2)
     pos_items = piece.shape[1]
     frame_n = piece.shape[2]
     flat = piece.reshape(pos_items * frame_n, feat_count)

time: 208 us -> 201 us (0.966)
  waiting for transfers between devices: 38.4 us -> 22.6 us
  blocking collectives: 41.4 us -> 51.5 us
  local copies, waits for them, and re-layouts: 70.2 us -> 66.1 us
  starting transfers between devices: 10.8 us -> 14.7 us
  matrix products: 43.7 us -> 40.8 us
    all_to_all x1 -> x0, waiting for transfers between devices: 36.3 us -> none  [shards(): lax.all_to_all(regrouped, 'tm', split_axis=0, concat_axis=2, tiled=True)]
    ppermute x0 -> x7, waiting for transfers between devices: none -> 20.5 us  [exchange_in_pairs(): lax.ppermute(sent, axis, [(i, i ^ hop) for i in range(size)])]
    ppermute x0 -> x7, starting transfers between devices: none -> 10.9 us  [exchange_in_pairs(): lax.ppermute(sent, axis, [(i, i ^ hop) for i in range(size)])]
    all_to_all x1, blocking collectives: 41.4 us -> 51.5 us  [shards(): lax.all_to_all(paired, ('tm', 'space'), split_axis=1, concat_axis=0, tile...]
    all_to_all x1 -> x0, starting transfers between devices: 7 us -> none  [shards(): lax.all_to_all(regrouped, 'tm', split_axis=0, concat_axis=2, tiled=True)]
    reshape x1 -> x0, local copies, waits for them, and re-layouts: 3.66 us -> none  [shards(): regrouped = regrouped.reshape(frame_count, span, 1, feat_count)]
    sub x2, matrix products: 16.4 us -> 13.7 us  [attend(): raised = jnp.exp(scores - row_max)]
    another operation x0 -> x2, local copies, waits for them, and re-layouts: none -> 2.51 us  [the longest x1 2.5 us: split_up(): array.reshape(*dims[:dim], size, dims[dim] // size, *dims[dim + 1:])]
  transfers between devices with their start and end apart: 2 -> 8, of which waited for: 2 -> 6; matrix products, arithmetic and copies ran while one was open for 0% -> 0% of each run, Pallas kernels for 0% -> 0%
where the time goes in v1:
time: 201 us; the launch traced here: 200 us
  local copies, waits for them, and re-layouts  66.1 us (33%)
  blocking collectives  51.5 us (26%)
  matrix products  40.8 us (20%)
  waiting for transfers between devices  22.6 us (11%)
  starting transfers between devices  14.7 us (7%)
  other arithmetic  4.35 us (2%)
    all_to_all x1, blocking collectives, shards(): lax.all_to_all(paired, ('tm', 'space'), split_axis=1, concat_axis=0, tile...  51.5 us
    ppermute x7, waiting for transfers between devices, exchange_in_pairs(): lax.ppermute(sent, axis, [(i, i ^ hop) for i in range(size)])  20.5 us
    unnamed x28, local copies, waits for them, and re-layouts  15.4 us
    sub x2, matrix products, attend(): raised = jnp.exp(scores - row_max)  13.7 us
    dot_general x2, matrix products, attend(): jnp.dot(normed, qkv_weight, preferred_element_type=jnp.float32)  11.8 us
    reshape x2, local copies, waits for them, and re-layouts, attend(): shaped = projected.reshape(blocks, per_block, 3, HEADS, HEAD)  11.5 us
    ppermute x7, starting transfers between devices, exchange_in_pairs(): lax.ppermute(sent, axis, [(i, i ^ hop) for i in range(size)])  10.9 us
    dot_general x2, matrix products, attend(): jnp.einsum('bhqk,bkhd->bqhd', weights, shaped[:, :, 2], preferred_element...  9.21 us
  transfers between devices with their start and end apart: 8, of which 6 were waited for; matrix products, arithmetic and copies ran while one was open for 0% of the time, Pallas kernels for 0%

profile of v1, /device:TPU:1, one launch (start us, length us, event | category | flops | bytes accessed | tf_op | source)
XLA Modules:
  0.0 200.4 jit_solution(3263938845058010887)
XLA Ops:
  0.0 2.7 %copy.92 = bf16[2,32,12,1024]{3,1,2,0:T(8,128)(2,1)} copy(bf16[2,32,12,1024]{3,1,0,2:T(8,128)(2,1)} %bitcast.193) | data formatting | bytes 3145728 | tf_op jit(solution)/shard_map/reshape | solution.py:76
  2.7 3.8 %all-to-all-start = ((bf16[2,32,12,1024]{3,1,2,0:T(8,128)(2,1)}), bf16[2,32,12,1024]{3,1,2,0:T(8,128)(2,1)S(1)}, u32[]{:S(2)}, u32[]{:S(2)}) async-start(bf16[2,32,12,1024]{3,1,2,0:T(8,128)(2,1)} %copy.92), calls=%async_computation | async-start | bytes 3145728 | tf_op jit(solution)/shard_map/all_to_all | solution.py:79
  6.6 2.1 %all-to-all-done = bf16[2,32,12,1024]{3,1,2,0:T(8,128)(2,1)S(1)} async-done(((bf16[2,32,12,1024]{3,1,2,0:T(8,128)(2,1)}), bf16[2,32,12,1024]{3,1,2,0:T(8,128)(2,1)S(1)}, u32[]{:S(2)}, u32[]{:S(2)}) %all-to-all-start) | async-done | bytes 1572896 | tf_op jit(solution)/shard_map/all_to_all | solution.py:79
  8.7 0.4 multiply_reduce_fusion.1
  9.1 0.0 copy-done.6
  9.1 0.4 multiply_convert_fusion.1
  9.5 2.2 %copy.94 = bf16[1,32,2,12,1024]{4,3,2,1,0:T(8,128)(2,1)} copy(bf16[1,32,2,12,1024]{4,1,3,2,0:T(8,128)(2,1)S(1)} %multiply_convert_fusion.1) | data formatting | bytes 3145728 | tf_op jit(solution)/shard_map/convert_element_type | solution.py:48
  11.8 2.5 %convert_element_type.80 = bf16[768,1024]{1,0:T(8,128)(2,1)S(1)} reshape(bf16[1,32,2,12,1024]{4,3,2,1,0:T(8,128)(2,1)} %copy.94) | data formatting | bytes 3145728 | tf_op jit(solution)/shard_map/convert_element_type | solution.py:48
  14.3 5.7 %convolution_convert_fusion.1 = bf16[768,1536]{1,0:T(8,128)(2,1)} fusion(bf16[768,1024]{1,0:T(8,128)(2,1)S(1)} %convert_element_type.80, bf16[2,1024,1536]{2,1,0:T(8,128)(2,1)} %param.6), kind=kOutput, calls=%fused_computation.20 | convolution fusion | flops 2417098752 | bytes 7077888 | tf_op jit(solution)/shard_map/dot_general | solution.py:49
  20.0 7.0 %reshape.183 = bf16[2,384,3,8,64]{4,3,2,1,0:T(8,128)(2,1)} reshape(bf16[768,1536]{1,0:T(8,128)(2,1)} %convolution_convert_fusion.1) | data formatting | bytes 4718592 | tf_op jit(solution)/shard_map/reshape | solution.py:52
  26.9 4.3 %fusion.66 = (bf16[2,384,1,8,64]{4,3,2,1,0:T(8,128)(2,1)S(1)}, bf16[2,384,1,8,64]{4,3,2,1,0:T(8,128)(2,1)}, bf16[2,384,1,8,64]{4,3,2,1,0:T(8,128)(2,1)}) fusion(bf16[2,384,3,8,64]{4,3,2,1,0:T(8,128)(2,1)} %reshape.183), kind=kLoop, calls=%fused_computation.98 | loop fusion | bytes 4718592 | tf_op jit(solution)/shard_map/slice | solution.py:63
  31.3 2.7 %copy.127 = bf16[2,384,1,8,64]{1,4,3,0,2:T(8,128)(2,1)} copy(bf16[2,384,1,8,64]{4,3,2,1,0:T(8,128)(2,1)} %get-tuple-element.9) | data formatting | bytes 1572864
  34.0 2.7 %copy.128 = bf16[2,384,1,8,64]{1,4,3,0,2:T(8,128)(2,1)} copy(bf16[2,384,1,8,64]{4,3,2,1,0:T(8,128)(2,1)} %get-tuple-element.10) | data formatting | bytes 1572864
  36.7 0.1 broadcast_compare_fusion.1
  36.8 1.7 copy.126
  38.5 8.2 %fusion.68 = (f32[2,8,384]{2,1,0:T(8,128)S(1)}, f32[2,8,384,384]{2,3,1,0:T(8,128)}) fusion(pred[384,384]{0,1:T(8,128)(4,1)S(1)} %broadcast_compare_fusion.1, bf16[2,384,1,8,64]{1,4,3,0,2:T(8,128)(2,1)} %copy.128, bf16[2,384,1,8,64]{1,4,3,0,2:T(8,128)(2,1)} %copy.127), kind=kOutput, calls=%fused_computation.100 | convolution fusion | flops 311427456 | bytes 11182080 | tf_op jit(solution)/shard_map/sub | solution.py:60
  46.7 0.0 copy-done.3
  46.7 4.5 %fusion.21 = bf16[2,384,8,64]{1,3,2,0:T(8,128)(2,1)S(1)} fusion(f32[2,8,384,384]{2,3,1,0:T(8,128)} %get-tuple-element.22, f32[2,8,384]{2,1,0:T(8,128)S(1)} %get-tuple-element.21, bf16[2,384,1,8,64]{1,4,3,0,2:T(8,128)(2,1)S(1)} %copy-done.3), kind=kOutput, calls=%fused_computation.39 | convolution fusion | flops 307101696 | bytes 11034624 | tf_op jit(solution)/shard_map/bhqk,bkhd->bqhd/dot_general | solution.py:62
  51.3 0.8 copy.100
  52.1 1.0 copy.132
  53.1 0.4 convert_bitcast_fusion.1
  53.5 3.8 %copy.93 = f32[1,32,2,12,1024]{4,3,2,1,0:T(8,128)} copy(f32[1,32,2,12,1024]{4,1,3,2,0:T(8,128)S(1)} %convert_bitcast_fusion.1) | data formatting | bytes 6291456 | tf_op jit(solution)/shard_map/convert_element_type | solution.py:45
  57.3 3.0 %reshape.162 = f32[768,1024]{1,0:T(8,128)S(1)} reshape(f32[1,32,2,12,1024]{4,3,2,1,0:T(8,128)} %copy.93) | data formatting | bytes 6291456 | tf_op jit(solution)/shard_map/convert_element_type | solution.py:45
  60.3 3.6 %add_convert_fusion = bf16[768,1024]{1,0:T(8,128)(2,1)} fusion(f32[768,1024]{1,0:T(8,128)S(1)} %reshape.162, bf16[768,512]{0,1:T(8,128)(2,1)} %bitcast.188, bf16[2,512,1024]{2,1,0:T(8,128)(2,1)} %param.7), kind=kOutput, calls=%fused_computation.30 | convolution fusion | flops 806879232 | bytes 6553600 | tf_op jit(solution)/shard_map/dot_general | solution.py:66
  63.9 2.5 %reshape_reshape.10 = bf16[32,2,12,1024]{3,2,1,0:T(8,128)(2,1)S(1)} reshape(bf16[768,1024]{1,0:T(8,128)(2,1)} %add_convert_fusion) | data formatting | bytes 3145728 | tf_op jit(solution)/shard_map/reshape;reshape | solution.py:85
  66.4 2.8 %copy.101 = bf16[32,12,2,1024]{3,2,1,0:T(2,128)(2,1)} copy(bf16[32,12,2,1024]{3,1,2,0:T(8,128)(2,1)S(1)} %bitcast.182) | data formatting | bytes 3145728 | tf_op jit(solution)/shard_map/transpose | solution.py:85
  69.2 2.5 %reshape_reshape.11 = bf16[8,1,96,1,1024]{4,2,0,3,1:T(8,128)(2,1)S(1)} reshape(bf16[32,12,2,1024]{3,2,1,0:T(2,128)(2,1)} %copy.101) | data formatting | bytes 3145728 | tf_op jit(solution)/shard_map/reshape;reshape | solution.py:12
  71.8 0.2 dynamic-slice_bitcast_fusion
  72.0 2.8 %collective-permute-start = (bf16[1,96,1,1024]{3,1,2,0:T(8,128)(2,1)S(1)}, bf16[1,96,1,1024]{3,1,2,0:T(8,128)(2,1)S(1)}, u32[]{:S(2)}, u32[]{:S(2)}) collective-permute-start(bf16[1,96,1,1024]{3,1,2,0:T(8,128)(2,1)S(1)} %get-tuple-element.17), channel_id=1, source_target_pairs={{0,2},{2,0},{4,6},{6,4},{8,10},{10,8},{12,14},{14,12},{1,3},{3,1},... | collective-permute-start | bytes 589832 | tf_op jit(solution)/shard_map/ppermute | solution.py:28
  74.7 1.3 collective-permute-start.1
  76.0 0.0 collective-permute-start.2
  76.0 2.4 %collective-permute-start.3 = (bf16[1,96,1,1024]{3,1,2,0:T(8,128)(2,1)S(1)}, bf16[1,96,1,1024]{3,1,2,0:T(8,128)(2,1)S(1)}, u32[]{:S(2)}, u32[]{:S(2)}) collective-permute-start(bf16[1,96,1,1024]{3,1,2,0:T(8,128)(2,1)S(1)} %get-tuple-element.14), channel_id=1, source_target_pairs={{0,8},{2,10},{4,12},{6,14},{8,0},{10,2},{12,4},{14,6},{1,9},{3,11}... | collective-permute-start | bytes 589832 | tf_op jit(solution)/shard_map/ppermute | solution.py:28
  78.5 1.0 collective-permute-start.4
  79.5 0.1 broadcast_compare_fusion
  79.6 0.0 collective-permute-done
  79.6 3.4 %collective-permute-start.5 = (bf16[1,96,1,1024]{3,1,2,0:T(8,128)(2,1)S(1)}, bf16[1,96,1,1024]{3,1,2,0:T(8,128)(2,1)S(1)}, u32[]{:S(2)}, u32[]{:S(2)}) collective-permute-start(bf16[1,96,1,1024]{3,1,2,0:T(8,128)(2,1)S(1)} %get-tuple-element.12), channel_id=1, source_target_pairs={{0,12},{2,14},{4,8},{6,10},{8,4},{10,6},{12,0},{14,2},{1,13},{3,15... | collective-permute-start | bytes 589832 | tf_op jit(solution)/shard_map/ppermute | solution.py:28
  83.0 5.1 %collective-permute-done.1 = bf16[1,96,1,1024]{3,1,2,0:T(8,128)(2,1)S(1)} collective-permute-done((bf16[1,96,1,1024]{3,1,2,0:T(8,128)(2,1)S(1)}, bf16[1,96,1,1024]{3,1,2,0:T(8,128)(2,1)S(1)}, u32[]{:S(2)}, u32[]{:S(2)}) %collective-permute-start.1) | collective-permute-done | bytes 196640 | tf_op jit(solution)/shard_map/ppermute | solution.py:28
  88.1 0.0 collective-permute-start.6
  88.1 3.7 %collective-permute-done.2 = bf16[1,96,1,1024]{3,1,2,0:T(8,128)(2,1)S(1)} collective-permute-done((bf16[1,96,1,1024]{3,1,2,0:T(8,128)(2,1)S(1)}, bf16[1,96,1,1024]{3,1,2,0:T(8,128)(2,1)S(1)}, u32[]{:S(2)}, u32[]{:S(2)}) %collective-permute-start.2) | collective-permute-done | bytes 196640 | tf_op jit(solution)/shard_map/ppermute | solution.py:28
  91.9 0.0 collective-permute-done.3
  91.9 0.4 collective-permute-done.4
  92.3 7.1 %collective-permute-done.5 = bf16[1,96,1,1024]{3,1,2,0:T(8,128)(2,1)S(1)} collective-permute-done((bf16[1,96,1,1024]{3,1,2,0:T(8,128)(2,1)S(1)}, bf16[1,96,1,1024]{3,1,2,0:T(8,128)(2,1)S(1)}, u32[]{:S(2)}, u32[]{:S(2)}) %collective-permute-start.5) | collective-permute-done | bytes 196640 | tf_op jit(solution)/shard_map/ppermute | solution.py:28
  99.5 4.2 %collective-permute-done.6 = bf16[1,96,1,1024]{3,1,2,0:T(8,128)(2,1)S(1)} collective-permute-done((bf16[1,96,1,1024]{3,1,2,0:T(8,128)(2,1)S(1)}, bf16[1,96,1,1024]{3,1,2,0:T(8,128)(2,1)S(1)}, u32[]{:S(2)}, u32[]{:S(2)}) %collective-permute-start.6) | collective-permute-done | bytes 196640 | tf_op jit(solution)/shard_map/ppermute | solution.py:28
  103.7 0.6 gather_fusion
  104.3 0.4 multiply_reduce_fusion
  104.7 2.0 %convert_bitcast_fusion = f32[1,96,8,1,1024]{4,1,2,3,0:T(8,128)} fusion(bf16[8,96,1024]{2,1,0:T(8,128)(2,1)S(1)} %gather_fusion), kind=kLoop, calls=%fused_computation.22 | loop fusion | flops 786432 | bytes 4718592 | tf_op jit(solution)/shard_map/convert_element_type | solution.py:45
  106.8 0.4 multiply_convert_fusion
  107.2 6.1 %convolution_convert_fusion = bf16[768,1536]{1,0:T(8,128)(2,1)S(1)} fusion(bf16[2,1024,1536]{2,1,0:T(8,128)(2,1)} %param.6, bf16[1,96,8,1,1024]{4,1,2,3,0:T(8,128)(2,1)S(1)} %multiply_convert_fusion), kind=kOutput, calls=%fused_computation.19 | convolution fusion | flops 2417098752 | bytes 7077888 | tf_op jit(solution)/shard_map/dot_general | solution.py:49
  113.3 4.5 %reshape.184 = bf16[2,384,3,8,64]{4,3,2,1,0:T(8,128)(2,1)} reshape(bf16[768,1536]{1,0:T(8,128)(2,1)S(1)} %convolution_convert_fusion) | data formatting | bytes 4718592 | tf_op jit(solution)/shard_map/reshape | solution.py:52
  117.8 3.8 %fusion.65 = (bf16[2,384,1,8,64]{4,3,2,1,0:T(8,128)(2,1)S(1)}, bf16[2,384,1,8,64]{4,3,2,1,0:T(8,128)(2,1)}, bf16[2,384,1,8,64]{4,3,2,1,0:T(8,128)(2,1)S(1)}) fusion(bf16[2,384,3,8,64]{4,3,2,1,0:T(8,128)(2,1)} %reshape.184), kind=kLoop, calls=%fused_computation.97 | loop fusion | bytes 4718592 | tf_op jit(solution)/shard_map/slice | solution.py:63
  121.6 2.7 %copy.130 = bf16[2,384,1,8,64]{1,4,3,0,2:T(8,128)(2,1)} copy(bf16[2,384,1,8,64]{4,3,2,1,0:T(8,128)(2,1)} %get-tuple-element.6) | data formatting | bytes 1572864
  124.3 1.7 copy.131
  126.0 1.7 copy.129
  127.7 5.5 %fusion.77 = (f32[2,8,384]{2,1,0:T(8,128)S(1)}, f32[2,8,384,384]{2,3,1,0:T(8,128)}) fusion(pred[384,384]{0,1:T(8,128)(4,1)S(1)} %broadcast_compare_fusion, bf16[2,384,1,8,64]{1,4,3,0,2:T(8,128)(2,1)S(1)} %copy-done.4, bf16[2,384,1,8,64]{1,4,3,0,2:T(8,128)(2,1)S(1)} %copy-done.2), kind=kOutput, calls=%fused_computation.101 | convolution fusion | flops 311427456 | bytes 11182080 | tf_op jit(solution)/shard_map/sub | solution.py:60
  133.3 4.7 %fusion.22 = bf16[2,384,8,64]{1,3,2,0:T(8,128)(2,1)S(1)} fusion(f32[2,8,384,384]{2,3,1,0:T(8,128)} %get-tuple-element.24, f32[2,8,384]{2,1,0:T(8,128)S(1)} %get-tuple-element.23, bf16[2,384,1,8,64]{1,4,3,0,2:T(8,128)(2,1)S(1)} %copy-done.5), kind=kOutput, calls=%fused_computation.40 | convolution fusion | flops 307101696 | bytes 11034624 | tf_op jit(solution)/shard_map/bhqk,bkhd->bqhd/dot_general | solution.py:62
  138.0 0.8 copy.116
  138.8 0.1 copy.133
  138.9 0.9 copy-done
  139.9 2.5 %fusion.13 = bf16[768,1024]{1,0:T(8,128)(2,1)S(1)} fusion(f32[1,96,8,1,1024]{4,1,2,3,0:T(8,128)S(1)} %copy-done, bf16[768,512]{0,1:T(8,128)(2,1)S(1)} %bitcast.189, bf16[2,512,1024]{2,1,0:T(8,128)(2,1)S(1)} %copy-done.1), kind=kOutput, calls=%fused_computation.24 | convolution fusion | flops 806879232 | bytes 6553600 | tf_op jit(solution)/shard_map/dot_general | solution.py:66
  142.3 0.9 copy.117
  143.2 51.5 %all_to_all.24 = bf16[48,16,1024]{2,0,1:T(8,128)(2,1)S(1)} all-to-all(bf16[48,16,1024]{2,0,1:T(8,128)(2,1)S(1)} %bitcast.184), channel_id=1, replica_groups=mesh['grp'=2,'tm'=8,'space'=2] {'tm','space'}, dimensions={1} | all-to-all | bytes 3145728 | tf_op jit(solution)/shard_map/all_to_all | solution.py:96
  194.7 1.3 copy.140
  196.0 2.4 %reshape.161 = bf16[64,12,1024]{2,1,0:T(8,128)(2,1)S(1)} reshape(bf16[2,8,48,1024]{3,2,1,0:T(8,128)(2,1)} %bitcast.186) | data formatting | bytes 3145728 | tf_op jit(solution)/shard_map/reshape | solution.py:100
  198.4 2.0 %copy.119 = bf16[1,12,64,1024]{3,2,1,0:T(8,128)(2,1)} copy(bf16[1,12,64,1024]{3,1,2,0:T(8,128)(2,1)S(1)} %bitcast.183) | data formatting | bytes 3145728 | tf_op jit(solution)/shard_map/broadcast_in_dim | solution.py:101
  (24 shorter events, 0.2 us)
Async XLA Ops:
  2.7 6.3 %copy-start.6 = (f32[2,1024]{1,0:T(2,128)S(1)}, f32[2,1024]{1,0:T(2,128)}, u32[]{:S(2)}) copy-start(f32[2,1024]{1,0:T(2,128)} %param.5) | copy-start | bytes 24580
  2.7 5.9 %all-to-all-start = ((bf16[2,32,12,1024]{3,1,2,0:T(8,128)(2,1)}), bf16[2,32,12,1024]{3,1,2,0:T(8,128)(2,1)S(1)}, u32[]{:S(2)}, u32[]{:S(2)}) async-start(bf16[2,32,12,1024]{3,1,2,0:T(8,128)(2,1)} %copy.92), calls=%async_computation | async-start | bytes 3145728 | tf_op jit(solution)/shard_map/all_to_all | solution.py:79
  38.5 8.2 %copy-start.3 = (bf16[2,384,1,8,64]{1,4,3,0,2:T(8,128)(2,1)S(1)}, bf16[2,384,1,8,64]{1,4,3,0,2:T(8,128)(2,1)}, u32[]{:S(2)}) copy-start(bf16[2,384,1,8,64]{1,4,3,0,2:T(8,128)(2,1)} %copy.126) | copy-start | bytes 2359300
  72.0 7.7 %collective-permute-start = (bf16[1,96,1,1024]{3,1,2,0:T(8,128)(2,1)S(1)}, bf16[1,96,1,1024]{3,1,2,0:T(8,128)(2,1)S(1)}, u32[]{:S(2)}, u32[]{:S(2)}) collective-permute-start(bf16[1,96,1,1024]{3,1,2,0:T(8,128)(2,1)S(1)} %get-tuple-element.17), channel_id=1, source_target_pairs={{0,2},{2,0},{4,6},{6,4},{8,10},{10,8},{12,14},{14,12},{1,3},{3,1},... | collective-permute-start | bytes 589832 | tf_op jit(solution)/shard_map/ppermute | solution.py:28
  74.7 13.4 %collective-permute-start.1 = (bf16[1,96,1,1024]{3,1,2,0:T(8,128)(2,1)S(1)}, bf16[1,96,1,1024]{3,1,2,0:T(8,128)(2,1)S(1)}, u32[]{:S(2)}, u32[]{:S(2)}) collective-permute-start(bf16[1,96,1,1024]{3,1,2,0:T(8,128)(2,1)S(1)} %get-tuple-element.16), channel_id=1, source_target_pairs={{0,4},{2,6},{4,0},{6,2},{8,12},{10,14},{12,8},{14,10},{1,5},{3,7},... | collective-permute-start | bytes 589832 | tf_op jit(solution)/shard_map/ppermute | solution.py:28
  76.0 15.8 %collective-permute-start.2 = (bf16[1,96,1,1024]{3,1,2,0:T(8,128)(2,1)S(1)}, bf16[1,96,1,1024]{3,1,2,0:T(8,128)(2,1)S(1)}, u32[]{:S(2)}, u32[]{:S(2)}) collective-permute-start(bf16[1,96,1,1024]{3,1,2,0:T(8,128)(2,1)S(1)} %get-tuple-element.15), channel_id=1, source_target_pairs={{0,6},{2,4},{4,2},{6,0},{8,14},{10,12},{12,10},{14,8},{1,7},{3,5},... | collective-permute-start | bytes 589832 | tf_op jit(solution)/shard_map/ppermute | solution.py:28
  76.0 15.8 %collective-permute-start.3 = (bf16[1,96,1,1024]{3,1,2,0:T(8,128)(2,1)S(1)}, bf16[1,96,1,1024]{3,1,2,0:T(8,128)(2,1)S(1)}, u32[]{:S(2)}, u32[]{:S(2)}) collective-permute-start(bf16[1,96,1,1024]{3,1,2,0:T(8,128)(2,1)S(1)} %get-tuple-element.14), channel_id=1, source_target_pairs={{0,8},{2,10},{4,12},{6,14},{8,0},{10,2},{12,4},{14,6},{1,9},{3,11}... | collective-permute-start | bytes 589832 | tf_op jit(solution)/shard_map/ppermute | solution.py:28
  78.5 13.8 %collective-permute-start.4 = (bf16[1,96,1,1024]{3,1,2,0:T(8,128)(2,1)S(1)}, bf16[1,96,1,1024]{3,1,2,0:T(8,128)(2,1)S(1)}, u32[]{:S(2)}, u32[]{:S(2)}) collective-permute-start(bf16[1,96,1,1024]{3,1,2,0:T(8,128)(2,1)S(1)} %get-tuple-element.13), channel_id=1, source_target_pairs={{0,10},{2,8},{4,14},{6,12},{8,2},{10,0},{12,6},{14,4},{1,11},{3,9}... | collective-permute-start | bytes 589832 | tf_op jit(solution)/shard_map/ppermute | solution.py:28
  79.6 19.8 %collective-permute-start.5 = (bf16[1,96,1,1024]{3,1,2,0:T(8,128)(2,1)S(1)}, bf16[1,96,1,1024]{3,1,2,0:T(8,128)(2,1)S(1)}, u32[]{:S(2)}, u32[]{:S(2)}) collective-permute-start(bf16[1,96,1,1024]{3,1,2,0:T(8,128)(2,1)S(1)} %get-tuple-element.12), channel_id=1, source_target_pairs={{0,12},{2,14},{4,8},{6,10},{8,4},{10,6},{12,0},{14,2},{1,13},{3,15... | collective-permute-start | bytes 589832 | tf_op jit(solution)/shard_map/ppermute | solution.py:28
  88.1 15.5 %collective-permute-start.6 = (bf16[1,96,1,1024]{3,1,2,0:T(8,128)(2,1)S(1)}, bf16[1,96,1,1024]{3,1,2,0:T(8,128)(2,1)S(1)}, u32[]{:S(2)}, u32[]{:S(2)}) collective-permute-start(bf16[1,96,1,1024]{3,1,2,0:T(8,128)(2,1)S(1)} %get-tuple-element.11), channel_id=1, source_target_pairs={{0,14},{2,12},{4,10},{6,8},{8,6},{10,4},{12,2},{14,0},{1,15},{3,13... | collective-permute-start | bytes 589832 | tf_op jit(solution)/shard_map/ppermute | solution.py:28
  126.0 1.7 copy-start.2
  126.0 1.7 copy-start.4
  127.7 5.5 %copy-start.5 = (bf16[2,384,1,8,64]{1,4,3,0,2:T(8,128)(2,1)S(1)}, bf16[2,384,1,8,64]{1,4,3,0,2:T(8,128)(2,1)}, u32[]{:S(2)}) copy-start(bf16[2,384,1,8,64]{1,4,3,0,2:T(8,128)(2,1)} %copy.129) | copy-start | bytes 2359300
  133.3 5.7 %copy-start.1 = (bf16[2,512,1024]{2,1,0:T(8,128)(2,1)S(1)}, bf16[2,512,1024]{2,1,0:T(8,128)(2,1)}, u32[]{:S(2)}) copy-start(bf16[2,512,1024]{2,1,0:T(8,128)(2,1)} %param.7) | copy-start | bytes 6291460
  138.0 1.9 copy-start
